TPU v7x, 32 devices: a whole 2x2x4 slice. The times are simulated.
32 devices in a mesh: tm: 16 (over z, y, x), rows: 2 (over core).
Axes of the slice: x: 2, y: 2, z: 4, core: 2. Of those that a mesh axis runs over, the one named last changes fastest.
Arguments:
- latents: bfloat16 [64, 8, 5120], P('tm', 'rows'), may hold values from -25 to 25
- cotangent: bfloat16 [64, 8, 5120], P('tm', 'rows'), may hold values from -6 to 6
- kernel_one: bfloat16 [3, 3, 3, 64, 64], replicated, may hold values from -0.15625 to 0.15625
- kernel_two: bfloat16 [3, 3, 3, 64, 64], replicated, may hold values from -0.15625 to 0.15625
- gain_one: float32 [64], replicated, may hold values from 0.5 to 1.5
- offset_one: float32 [64], replicated, may hold values from -3 to 3
- gain_two: float32 [64], replicated, may hold values from 0.5 to 1.5
- offset_two: float32 [64], replicated, may hold values from -3 to 3
- clip_id: int32 [64], P('tm'), may hold values from 0 to 7, never falling along the last dimension, each value on 1 to 16 neighbouring positions
Outputs:
- output: bfloat16 [64, 8, 5120], P('tm', 'rows')
- grad_latent: bfloat16 [64, 8, 5120], P('tm', 'rows')
- grad_kernel_one: float32 [3, 3, 3, 64, 64], replicated
- grad_kernel_two: float32 [3, 3, 3, 64, 64], replicated
Inputs may be any that keep to these rules, and one draw needn't show every extreme that they name: `clip_id`: clip numbers never fall along the frames; each clip number 0 to 7 names 1 to 16 consecutive frames, and one clip has exactly 16.
All inputs are finite; a program needn't handle non-finite values.
Results may differ from a plain program's by a relative error of at most 0.0085.
Values may be sent and summed in bfloat16 or wider, within the bound.
A program may use at most 128 MiB of HBM per device.

v0:
```python
import jax
import jax.numpy as jnp
from jax import lax
from jax.sharding import PartitionSpec as P

GROUPS = 32


EPSILON = 1e-06
HIGHEST = lax.Precision.HIGHEST


def with_halo(block, sides, width):
    for axis, dim in sides:
        count = lax.axis_size(axis)
        forward = [(i, i + 1) for i in range(count - 1)]
        backward = [(target, source) for source, target in forward]
        low = lax.ppermute(
            lax.slice_in_dim(block, block.shape[dim] - width, None, axis=dim), axis, forward
        )
        high = lax.ppermute(lax.slice_in_dim(block, 0, width, axis=dim), axis, backward)
        block = jnp.concatenate([low, block, high], axis=dim)
    return block


def passed_along(value, axis, by):
    length = lax.axis_size(axis)
    pairs = [(i, i + by) for i in range(length) if 0 <= i + by < length]
    return lax.ppermute(value, axis, pairs)


def row_halo(extended):
    return with_halo(extended, (("rows", 1),), 1)


def spread(extended, channels):
    depth, height, flat = extended.shape
    shaped = extended.reshape(depth, height, flat // channels, channels)
    return jnp.pad(shaped, ((0, 0), (0, 0), (1, 1), (0, 0)))


def forward_taps(frames, n_rows, n_cols):
    taps = [
        frames[:, row_tap : row_tap + n_rows, col_tap : col_tap + n_cols]
        for row_tap in range(3)
        for col_tap in range(3)
    ]
    joined = jnp.concatenate(taps, axis=-1)
    return joined.reshape(-1, joined.shape[-1])


def reverse_taps(frames, n_rows, n_cols):
    taps = [
        frames[:, 2 - row_tap : 2 - row_tap + n_rows, 2 - col_tap : 2 - col_tap + n_cols]
        for row_tap in range(3)
        for col_tap in range(3)
    ]
    joined = jnp.concatenate(taps, axis=-1)
    return joined.reshape(-1, joined.shape[-1])


def causal_conv(field, tags, kernel):
    n_frames, n_rows, flat = field.shape
    channels = kernel.shape[3]
    n_cols = flat // channels
    past_field, past_tags = passed_along((field[-2:], tags[-2:]), "tm", 1)
    padded = spread(row_halo(jnp.concatenate([past_field, field], axis=0)), channels)
    all_tags = jnp.concatenate([past_tags, tags])
    result = jnp.zeros((n_frames * n_rows * n_cols, kernel.shape[4]), jnp.float32)
    patch_list = []
    for lag in range(3):
        lag_mask = (all_tags[2 - lag : 2 - lag + n_frames] == tags).astype(jnp.bfloat16)
        frames = padded[2 - lag : 2 - lag + n_frames] * lag_mask[:, None, None, None]
        patches = forward_taps(frames, n_rows, n_cols)
        patch_list.append(patches)
        result = result + jnp.dot(
            patches, kernel[lag].reshape(-1, kernel.shape[4]), preferred_element_type=jnp.float32
        )
    return (result.reshape(n_frames, n_rows, flat), patch_list)


def transposed_conv(grad, tags, kernel):
    n_frames, n_rows, flat = grad.shape
    channels = kernel.shape[3]
    n_cols = flat // channels
    next_grad, next_tags = passed_along((grad[:2], tags[:2]), "tm", -1)
    padded = spread(row_halo(jnp.concatenate([grad, next_grad], axis=0)), channels)
    all_tags = jnp.concatenate([tags, next_tags])
    result = jnp.zeros((n_frames * n_rows * n_cols, channels), jnp.float32)
    for lag in range(3):
        lag_mask = (all_tags[lag : lag + n_frames] == tags).astype(jnp.bfloat16)
        frames = padded[lag : lag + n_frames] * lag_mask[:, None, None, None]
        patches = reverse_taps(frames, n_rows, n_cols)
        flipped = jnp.swapaxes(kernel[lag], 2, 3).reshape(-1, channels)
        result = result + jnp.dot(patches, flipped, preferred_element_type=jnp.float32)
    return result.reshape(n_frames, n_rows, flat)


def kernel_grad(patch_list, grad, channels):
    flat_grad = grad.reshape(-1, channels)
    stacked = [
        lax.dot_general(
            patches, flat_grad, (((0,), (0,)), ((), ())), preferred_element_type=jnp.float32
        ).reshape(3, 3, channels, channels)
        for patches in patch_list
    ]
    return jnp.stack(stacked)


def clip_totals(first, second, ones_col, clip_id):
    clips = lax.axis_size("tm") // 2
    onehot = (clip_id[:, None] == jnp.arange(clips, dtype=jnp.int32)[None, :]).astype(jnp.float32)
    table_a = jnp.dot(onehot.T, first, precision=HIGHEST)
    table_b = jnp.dot(onehot.T, second, precision=HIGHEST)
    table_c = jnp.dot(onehot.T, ones_col, precision=HIGHEST)
    summed_a, summed_b, summed_c = lax.psum((table_a, table_b, table_c), ("tm", "rows"))
    return (
        jnp.dot(onehot, summed_a, precision=HIGHEST),
        jnp.dot(onehot, summed_b, precision=HIGHEST),
        jnp.dot(onehot, summed_c, precision=HIGHEST),
    )


def norm_forward(field, gain, offset, clip_id):
    n_frames, n_rows, flat = field.shape
    channels = gain.shape[0]
    per_group = channels // GROUPS
    grouped = field.reshape(n_frames, n_rows * (flat // channels), GROUPS, per_group)
    first = jnp.sum(grouped, axis=(1, 3))
    second = jnp.sum(grouped * grouped, axis=(1, 3))
    ones_col = jnp.ones((n_frames, 1), jnp.float32)
    total_a, total_b, total_c = clip_totals(first, second, ones_col, clip_id)
    cells_count = total_c * float(grouped.shape[1] * per_group)
    mean_val = total_a / cells_count
    square_mean = total_b / cells_count
    inv_std = lax.rsqrt(square_mean - mean_val * mean_val + EPSILON)
    normed = (grouped - mean_val[:, None, :, None]) * inv_std[:, None, :, None]
    z_value = normed * gain.reshape(1, 1, GROUPS, per_group) + offset.reshape(
        1, 1, GROUPS, per_group
    )
    return (normed, z_value, inv_std, cells_count)


def norm_backward(grad, normed, z_value, inv_std, cells_count, gain, clip_id):
    per_group = normed.shape[3]
    grouped_grad = grad.reshape(normed.shape)
    sigmoid_z = jax.nn.sigmoid(z_value)
    grad_norm = (
        grouped_grad
        * sigmoid_z
        * (1.0 + z_value * (1.0 - sigmoid_z))
        * gain.reshape(1, 1, GROUPS, per_group)
    )
    first = jnp.sum(grad_norm, axis=(1, 3))
    second = jnp.sum(grad_norm * normed, axis=(1, 3))
    ones_col = jnp.ones((normed.shape[0], 1), jnp.float32)
    total_a, total_b, total_c = clip_totals(first, second, ones_col, clip_id)
    p_term = total_a / cells_count
    q_term = total_b / cells_count
    result = inv_std[:, None, :, None] * (
        grad_norm - p_term[:, None, :, None] - normed * q_term[:, None, :, None]
    )
    return result.reshape(grad.shape)


def per_device(
    latents, cotangent, kernel_one, kernel_two, gain_one, offset_one, gain_two, offset_two, clip_id
):
    channels = gain_one.shape[0]
    tags = (clip_id + 1).astype(jnp.bfloat16)
    field = latents.astype(jnp.float32)
    normed_one, z_one, inv_one, cells_count = norm_forward(field, gain_one, offset_one, clip_id)
    act_one = jax.nn.silu(z_one).astype(jnp.bfloat16).reshape(latents.shape)
    conv_one, patches_one = causal_conv(act_one, tags, kernel_one)
    hidden = conv_one.astype(jnp.bfloat16)
    normed_two, z_two, inv_two, count_again = norm_forward(
        hidden.astype(jnp.float32), gain_two, offset_two, clip_id
    )
    act_two = jax.nn.silu(z_two).astype(jnp.bfloat16).reshape(latents.shape)
    conv_two, patches_two = causal_conv(act_two, tags, kernel_two)
    output = (field + conv_two).astype(jnp.bfloat16)
    grad_two = kernel_grad(patches_two, cotangent, channels)
    back_two = transposed_conv(cotangent, tags, kernel_two)
    grad_hidden = norm_backward(
        back_two, normed_two, z_two, inv_two, count_again, gain_two, clip_id
    ).astype(jnp.bfloat16)
    grad_one = kernel_grad(patches_one, grad_hidden, channels)
    back_one = transposed_conv(grad_hidden, tags, kernel_one)
    branch = norm_backward(back_one, normed_one, z_one, inv_one, cells_count, gain_one, clip_id)
    grad_latent = (cotangent.astype(jnp.float32) + branch).astype(jnp.bfloat16)
    grad_one, grad_two = lax.psum((grad_one, grad_two), ("tm", "rows"))
    return (output, grad_latent, grad_one, grad_two)


def solution(mesh):
    return jax.shard_map(
        per_device,
        mesh=mesh,
        in_specs=(
            P("tm", "rows", None),
            P("tm", "rows", None),
            P(),
            P(),
            P(),
            P(),
            P(),
            P(),
            P("tm"),
        ),
        out_specs=(P("tm", "rows", None), P("tm", "rows", None), P(), P()),
        check_vma=False,
    )
```

profile of v0, /device:TPU:0, one launch (start us, length us, event | category | flops | bytes accessed | tf_op | source)
XLA Modules:
  0.0 727.6 jit_solution(2860579713837529750)
XLA Ops:
  23.4 11.2 %fusion.74 = (f32[4,32]{0,1:T(8,128)S(1)}, f32[4,32]{0,1:T(8,128)S(1)}) fusion(f32[4,320,32,2]{0,3,2,1:T(2,128)} %bitcast.178), kind=kLoop, calls=%fused_computation.168 | loop fusion | flops 245504 | bytes 328704 | tf_op jit(solution)/shard_map/reduce_sum | solution.py:129
  34.7 10.2 %copy.295 = f32[4,320,32,2]{1,2,3,0:T(8,128)S(1)} copy(f32[4,320,32,2]{0,3,2,1:T(2,128)} %bitcast.179) | data formatting | bytes 655360 | tf_op jit(solution)/shard_map/reshape | solution.py:128
  45.8 45.0 %all-reduce.7 = (f32[8,32]{1,0:T(8,128)S(1)}, f32[8,32]{1,0:T(8,128)S(1)}, f32[8]{0:T(128)S(1)}) all-reduce(f32[8,32]{1,0:T(8,128)S(1)} %fusion.49, f32[8,32]{1,0:T(8,128)S(1)} %fusion.51, f32[8]{0:T(128)S(1)} %convolution_bitcast_fusion.7), channel_id=1, replica_groups=mesh['tm'=16,'rows'=2] {'tm','rows'}, use_global_device_ids=true, to_apply=%region_4.0 | all-reduce | flops 520 | bytes 4160 | tf_op jit(solution)/shard_map/psum | solution.py:116
  92.5 6.1 copy.298
  98.6 11.6 %slice.451 = bf16[2,4,5120]{2,1,0:T(4,128)(2,1)S(1)} reshape(bf16[2,320,32,2]{3,2,1,0:T(8,128)(2,1)} %copy.298) | data formatting | bytes 163840 | tf_op jit(solution)/shard_map/slice | solution.py:66
  125.3 6.8 add.169
  136.3 6.8 mul.339
  147.8 6.8 add.156
  157.5 6.8 mul.318
  164.3 6.1 sub.92.clone
  176.5 6.1 mul.309.clone
  266.2 39.8 %all-reduce.6 = (f32[8,32]{1,0:T(8,128)S(1)}, f32[8,32]{1,0:T(8,128)S(1)}) all-reduce(f32[8,32]{1,0:T(8,128)S(1)} %fusion.45, f32[8,32]{1,0:T(8,128)S(1)} %fusion.47), channel_id=1, replica_groups=mesh['tm'=16,'rows'=2] {'tm','rows'}, use_global_device_ids=true, to_apply=%region_8.9 | all-reduce | flops 512 | bytes 4096 | tf_op jit(solution)/shard_map/psum | solution.py:116
  312.9 39.9 %all-reduce.5 = (f32[8,32]{1,0:T(8,128)S(1)}, f32[8,32]{1,0:T(8,128)S(1)}) all-reduce(f32[8,32]{1,0:T(8,128)S(1)} %fusion.41, f32[8,32]{1,0:T(8,128)S(1)} %fusion.43), channel_id=1, replica_groups=mesh['tm'=16,'rows'=2] {'tm','rows'}, use_global_device_ids=true, to_apply=%region_12.13 | all-reduce | flops 512 | bytes 4096 | tf_op jit(solution)/shard_map/psum | solution.py:116
  360.2 6.1 copy.310
  366.3 11.5 %slice.491 = bf16[2,4,5120]{2,1,0:T(4,128)(2,1)S(1)} reshape(bf16[2,320,32,2]{3,2,1,0:T(8,128)(2,1)} %copy.310) | data formatting | bytes 163840 | tf_op jit(solution)/shard_map/slice | solution.py:66
  382.2 6.2 sub.104
  394.4 6.2 mul.360
  406.6 6.2 mul.330.clone
  418.8 6.2 sub.97.clone
  487.5 41.4 %all-reduce.4 = (f32[8,32]{1,0:T(8,128)S(1)}, f32[8,32]{1,0:T(8,128)S(1)}) all-reduce(f32[8,32]{1,0:T(8,128)S(1)} %fusion.37, f32[8,32]{1,0:T(8,128)S(1)} %fusion.39), channel_id=1, replica_groups=mesh['tm'=16,'rows'=2] {'tm','rows'}, use_global_device_ids=true, to_apply=%region_16.17 | all-reduce | flops 512 | bytes 4096 | tf_op jit(solution)/shard_map/psum | solution.py:116
  559.7 6.1 mul.376
  571.8 6.1 sub.110
  578.0 6.1 copy.344
  587.0 130.3 %all-reduce.11.cloned.1.call-done = (f32[3,3,3,64,64]{4,3,2,1,0:T(8,128)}, f32[3,3,3,64,64]{4,3,2,1,0:T(8,128)}) async-done(((f32[3,3,3,64,64]{4,3,2,1,0:T(8,128)}, f32[3,3,3,64,64]{4,3,2,1,0:T(8,128)}), (f32[3,3,3,64,64]{4,3,2,1,0:T(8,128)}, f32[3,3,3,64,64]{4,3,2,1,0:T(8,128)})) %all-reduce.11.cloned.1.call-update) | async-done | bytes 884752 | tf_op jit(solution)/shard_map/psum | solution.py:191
  (359 shorter events, 276.5 us)
Async XLA Ops:
  7.2 710.2 %all-reduce.11.cloned.1.call-start = ((), (), s32[]{:S(2)}) async-start(), calls=%async_computation | async-start | bytes 3538944 | tf_op jit(solution)/shard_map/psum | solution.py:191
  7.9 181.0 %collective-permute-start.10 = (bf16[2]{0:T(256)(128)(2,1)S(1)}, bf16[2]{0:T(256)(128)(2,1)S(1)}, u32[]{:S(2)}, u32[]{:S(2)}) collective-permute-start(bf16[2]{0:T(256)(128)(2,1)S(1)} %get-tuple-element.192), channel_id=1, source_target_pairs={{2,0},{4,2},{6,4},{8,6},{10,8},{12,10},{14,12},{16,14},{18,16},{20... | collective-permute-start | bytes 20 | tf_op jit(solution)/shard_map/ppermute | solution.py:29
  9.2 179.8 %collective-permute-start.3 = (bf16[2]{0:T(256)(128)(2,1)S(1)}, bf16[2]{0:T(256)(128)(2,1)S(1)}, u32[]{:S(2)}, u32[]{:S(2)}) collective-permute-start(bf16[2]{0:T(256)(128)(2,1)S(1)} %get-tuple-element.193), channel_id=1, source_target_pairs={{0,2},{2,4},{4,6},{6,8},{8,10},{10,12},{12,14},{14,16},{16,18},{18... | collective-permute-start | bytes 20 | tf_op jit(solution)/shard_map/ppermute | solution.py:29
  15.6 173.6 %collective-permute-start.7 = (bf16[2,4,5120]{2,1,0:T(4,128)(2,1)S(1)}, bf16[2,4,5120]{2,1,0:T(4,128)(2,1)S(1)}, u32[]{:S(2)}, u32[]{:S(2)}) collective-permute-start(bf16[2,4,5120]{2,1,0:T(4,128)(2,1)S(1)} %slice.527), channel_id=1, source_target_pairs={{2,0},{4,2},{6,4},{8,6},{10,8},{12,10},{14,12},{16,14},{18,16},{20... | collective-permute-start | bytes 245768 | tf_op jit(solution)/shard_map/ppermute | solution.py:29
  44.9 53.7 %copy-start.11 = (f32[4,320,32,2]{1,2,3,0:T(8,128)}, f32[4,320,32,2]{1,2,3,0:T(8,128)S(1)}, u32[]{:S(2)}) copy-start(f32[4,320,32,2]{1,2,3,0:T(8,128)S(1)} %copy.295) | copy-start | bytes 983044
  45.1 46.6 %copy-start.55 = (f32[32,2]{0,1:T(2,128)}, f32[32,2]{0,1:T(2,128)S(1)}, u32[]{:S(2)}) copy-start(f32[32,2]{0,1:T(2,128)S(1)} %copy.296) | copy-start | bytes 772
  91.0 262.0 %copy-start.73 = (f32[4]{0:T(128)}, f32[4]{0:T(128)S(1)}, u32[]{:S(2)}) copy-start(f32[4]{0:T(128)S(1)} %fusion.8) | copy-start | bytes 52
  110.2 81.8 %collective-permute-start = (bf16[2,4,5120]{2,1,0:T(4,128)(2,1)S(1)}, bf16[2,4,5120]{2,1,0:T(4,128)(2,1)S(1)}, u32[]{:S(2)}, u32[]{:S(2)}) collective-permute-start(bf16[2,4,5120]{2,1,0:T(4,128)(2,1)S(1)} %slice.451), channel_id=1, source_target_pairs={{0,2},{2,4},{4,6},{6,8},{8,10},{10,12},{12,14},{14,16},{16,18},{18... | collective-permute-start | bytes 245768 | tf_op jit(solution)/shard_map/ppermute | solution.py:29
  154.6 34.1 %copy-start.36 = (f32[4,5120]{1,0:T(4,128)}, f32[4,5120]{1,0:T(4,128)S(1)}, u32[]{:S(2)}) copy-start(f32[4,5120]{1,0:T(4,128)S(1)} %add.156) | copy-start | bytes 245764
  189.4 7.4 %collective-permute-start.8 = (bf16[6,1,5120]{2,1,0:T(2,128)(2,1)S(1)}, bf16[6,1,5120]{2,1,0:T(2,128)(2,1)S(1)}, u32[]{:S(2)}, u32[]{:S(2)}) collective-permute-start(bf16[6,1,5120]{2,1,0:T(2,128)(2,1)S(1)} %get-tuple-element.177), channel_id=1, source_target_pairs={{0,1},{2,3},{4,5},{6,7},{8,9},{10,11},{12,13},{14,15},{16,17},{18,... | collective-permute-start | bytes 184328 | tf_op jit(solution)/shard_map/ppermute | solution.py:18
  190.7 6.1 collective-permute-start.9
  192.3 5.5 collective-permute-start.2
  193.8 4.1 collective-permute-start.1
  265.5 43.4 %copy-start.17 = (f32[1280,64]{1,0:T(8,128)S(1)}, f32[1280,64]{1,0:T(8,128)}, u32[]{:S(2)}) copy-start(f32[1280,64]{1,0:T(8,128)} %copy.311) | copy-start | bytes 983044
  312.1 43.6 %copy-start.7 = (f32[1280,64]{0,1:T(8,128)S(1)}, f32[1280,64]{0,1:T(8,128)}, u32[]{:S(2)}) copy-start(f32[1280,64]{0,1:T(8,128)} %fusion.1) | copy-start | bytes 983044
  312.1 43.6 %copy-start.9 = (f32[1280,64]{0,1:T(8,128)S(1)}, f32[1280,64]{0,1:T(8,128)}, u32[]{:S(2)}) copy-start(f32[1280,64]{0,1:T(8,128)} %copy-done.8) | copy-start | bytes 983044
  312.1 43.6 %copy-start.29 = (f32[1280,64]{0,1:T(8,128)S(1)}, f32[1280,64]{0,1:T(8,128)}, u32[]{:S(2)}) copy-start(f32[1280,64]{0,1:T(8,128)} %sub.114) | copy-start | bytes 983044
  377.9 64.6 %collective-permute-start.4 = (bf16[2,4,5120]{2,1,0:T(4,128)(2,1)S(1)}, bf16[2,4,5120]{2,1,0:T(4,128)(2,1)S(1)}, u32[]{:S(2)}, u32[]{:S(2)}) collective-permute-start(bf16[2,4,5120]{2,1,0:T(4,128)(2,1)S(1)} %slice.491), channel_id=1, source_target_pairs={{0,2},{2,4},{4,6},{6,8},{8,10},{10,12},{12,14},{14,16},{16,18},{18... | collective-permute-start | bytes 245768 | tf_op jit(solution)/shard_map/ppermute | solution.py:29
  431.5 6.3 collective-permute-start.11
  438.2 10.9 %collective-permute-start.13 = (bf16[6,1,5120]{2,0,1:T(8,128)(2,1)S(1)}, bf16[6,1,5120]{2,0,1:T(8,128)(2,1)S(1)}, u32[]{:S(2)}, u32[]{:S(2)}) collective-permute-start(bf16[6,1,5120]{2,0,1:T(8,128)(2,1)S(1)} %copy.334), channel_id=1, source_target_pairs={{1,0},{3,2},{5,4},{7,6},{9,8},{11,10},{13,12},{15,14},{17,16},{19,... | collective-permute-start | bytes 184328 | tf_op jit(solution)/shard_map/ppermute | solution.py:21
  439.5 9.7 %collective-permute-start.12 = (bf16[6,1,5120]{2,0,1:T(8,128)(2,1)S(1)}, bf16[6,1,5120]{2,0,1:T(8,128)(2,1)S(1)}, u32[]{:S(2)}, u32[]{:S(2)}) collective-permute-start(bf16[6,1,5120]{2,0,1:T(8,128)(2,1)S(1)} %copy.333), channel_id=1, source_target_pairs={{0,1},{2,3},{4,5},{6,7},{8,9},{10,11},{12,13},{14,15},{16,17},{18,... | collective-permute-start | bytes 184328 | tf_op jit(solution)/shard_map/ppermute | solution.py:18
  443.5 31.8 %collective-permute-start.6 = (bf16[6,1,5120]{2,0,1:T(8,128)(2,1)}, bf16[6,1,5120]{2,0,1:T(8,128)(2,1)}, u32[]{:S(2)}, u32[]{:S(2)}) collective-permute-start(bf16[6,1,5120]{2,0,1:T(8,128)(2,1)} %copy.379), channel_id=1, source_target_pairs={{1,0},{3,2},{5,4},{7,6},{9,8},{11,10},{13,12},{15,14},{17,16},{19,... | collective-permute-start | bytes 184328 | tf_op jit(solution)/shard_map/ppermute | solution.py:21
  444.8 31.5 %collective-permute-start.5 = (bf16[6,1,5120]{2,0,1:T(8,128)(2,1)S(1)}, bf16[6,1,5120]{2,0,1:T(8,128)(2,1)}, u32[]{:S(2)}, u32[]{:S(2)}) collective-permute-start(bf16[6,1,5120]{2,0,1:T(8,128)(2,1)S(1)} %copy.378), channel_id=1, source_target_pairs={{0,1},{2,3},{4,5},{6,7},{8,9},{10,11},{12,13},{14,15},{16,17},{18,... | collective-permute-start | bytes 184328 | tf_op jit(solution)/shard_map/ppermute | solution.py:18
  484.0 44.9 %copy-start.74 = (f32[4]{0:T(128)S(1)}, f32[4]{0:T(128)}, u32[]{:S(2)}) copy-start(f32[4]{0:T(128)} %copy-done.73) | copy-start | bytes 52
  (66 other events, 409.5 us)
Sparse Core Ops, SparseCore 0:
  585.3 132.0 all-reduce.10
where the time goes:
time: 739 us; the launch traced here: 728 us
  local copies, waits for them, and re-layouts  314 us (42%)
  blocking collectives  166 us (22%)
  waiting for transfers between devices  134 us (18%)
  matrix products  38 us (5%)
  starting transfers between devices  35.2 us (5%)
  other arithmetic  24.3 us (3%)
  between operations  15.6 us (2%)
    psum x4, blocking collectives, clip_totals(): lax.psum((table_a, table_b, table_c), ('tm', 'rows'))  166 us
    psum x1, waiting for transfers between devices, per_device(): grad_one, grad_two = lax.psum((grad_one, grad_two), ('tm', 'rows'))  130 us
    slice x4, local copies, waits for them, and re-layouts, causal_conv(): past_field, past_tags = passed_along((field[-2:], tags[-2:]), 'tm', 1)  35.3 us
    concatenate x6, local copies, waits for them, and re-layouts, forward_taps(): joined = jnp.concatenate(taps, axis=-1)  26.6 us
    sub x6, local copies, waits for them, and re-layouts, norm_backward(): grad_norm - p_term[:, None, :, None] - normed * q_term[:, None, :, None]  25.6 us
    mul x6, local copies, waits for them, and re-layouts, norm_forward(): normed = (grouped - mean_val[:, None, :, None]) * inv_std[:, None, :, None]  25.5 us
    sub x6, local copies, waits for them, and re-layouts, norm_forward(): normed = (grouped - mean_val[:, None, :, None]) * inv_std[:, None, :, None]  25.5 us
    mul x6, local copies, waits for them, and re-layouts, norm_backward(): normed * q_term[:, None, :, None]  25.4 us
  transfers between devices with their start and end apart: 15, of which 2 were waited for; matrix products, arithmetic and copies ran while one was open for 28% of the time, Pallas kernels for 0%

commit v1 on v0

v1 whole, which is shorter than its diff:
```python
import functools
import jax
import jax.numpy as jnp
from jax import lax
from jax.experimental import pallas as pl
from jax.experimental.pallas import tpu as pltpu
from jax.sharding import PartitionSpec as P

EPSILON = 1e-06
REACH = 4
SLOTS = 2 * (2 * REACH + 1)
OWN = 2 * REACH
PAIRS = 48
PIECES = 27
ALL = 32
MESH = pl.DeviceIdType.MESH
F32 = jnp.float32
BF16 = jnp.bfloat16


def kernel(
    n_tm, n_cols, lat_ref, cot_ref, ids_ref, w1_ref, w1t_ref, w2_ref, w2t_ref, vec_ref,
    out_ref, gl_ref, g1_ref, g2_ref,
    lat, cot, hid, err, stats, win_one, win_two, win_cot, win_back,
    stat_send, stat_recv, halo_send, halo_recv, *shared,
):
    direct = len(shared) > 0
    me = lax.axis_index("tm")
    core = lax.axis_index("rows")
    cells = 16 * PAIRS

    def within(d):
        if d == 0:
            return None
        return me + d < n_tm if d > 0 else me + d >= 0

    def guarded(cond, fn):
        if cond is None:
            fn()
        else:
            pl.when(cond)(fn)

    peers = [
        (d, o) for d in range(-REACH, REACH + 1) for o in range(2) if (d, o) != (0, 0)
    ]

    def device(d, o):
        return (me + d, core if o == 0 else 1 - core)

    def stat_copy(turn, d, o):
        slot = (REACH - d) * 2 + o
        return pltpu.make_async_remote_copy(
            src_ref=stats.at[turn, OWN],
            dst_ref=stats.at[turn, slot],
            send_sem=stat_send.at[turn, slot],
            recv_sem=stat_recv.at[turn, slot],
            device_id=device(d, o),
            device_id_type=MESH,
        )

    def send_stats(turn):
        for d, o in peers:
            guarded(within(d), lambda d=d, o=o: stat_copy(turn, d, o).start())

    def recv_stats(turn):
        for d, o in peers:
            guarded(within(-d), lambda d=d, o=o: stat_copy(turn, d, o).wait_recv())

    row_from = 4 - 3 * core
    row_to = 5 * core
    spans = {"past": (1, 4, 0, 2), "here": (0, 2, 2, 4), "next": (-1, 2, 6, 2)}

    def halo_copy(index, buf, kind, o):
        d, start, to, size = spans[kind]
        if o == 0:
            src = buf.at[pl.ds(start, size), pl.ds(1, 4)]
            dst = buf.at[pl.ds(to, size), pl.ds(1, 4)]
        else:
            src = buf.at[pl.ds(start, size), pl.ds(row_from, 1)]
            dst = buf.at[pl.ds(to, size), pl.ds(row_to, 1)]
        return pltpu.make_async_remote_copy(
            src_ref=src,
            dst_ref=dst,
            send_sem=halo_send.at[index],
            recv_sem=halo_recv.at[index],
            device_id=device(d, o),
            device_id_type=MESH,
        )

    halos = {
        "lat": [(0, lat, "past", 0), (1, lat, "past", 1), (2, lat, "here", 1)],
        "cot": [(3, cot, "next", 0), (4, cot, "next", 1), (5, cot, "here", 1)],
        "err": [(6, err, "next", 0), (7, err, "next", 1), (8, err, "here", 1)],
        "hid": [
            (9, hid, "past", 0), (10, hid, "past", 1), (11, hid, "here", 1),
            (12, hid, "next", 0), (13, hid, "next", 1),
        ],
    }

    def send_halo(name):
        for item in halos[name]:
            guarded(within(spans[item[2]][0]), lambda item=item: halo_copy(*item).start())

    def recv_halo(name):
        for item in halos[name]:
            guarded(
                within(-spans[item[2]][0]), lambda item=item: halo_copy(*item).wait_recv()
            )

    rank = 2 * me + core

    def around(step):
        target = (rank + step) % ALL
        return (target // 2, target % 2)

    def scatter_copy(which, step):
        parts, landing, sums, send, recv = shared[5 * which : 5 * which + 5]
        return pltpu.make_async_remote_copy(
            src_ref=parts.at[(rank + step) % ALL],
            dst_ref=landing.at[step],
            send_sem=send.at[0, step],
            recv_sem=recv.at[0, step],
            device_id=around(step),
            device_id_type=MESH,
        )

    def gather_copy(which, step):
        parts, landing, sums, send, recv = shared[5 * which : 5 * which + 5]
        return pltpu.make_async_remote_copy(
            src_ref=sums.at[rank],
            dst_ref=sums.at[rank],
            send_sem=send.at[1, step],
            recv_sem=recv.at[1, step],
            device_id=around(step),
            device_id_type=MESH,
        )

    owner = rank < PIECES

    def scatter(which):
        for step in range(1, ALL):
            pl.when((rank + step) % ALL < PIECES)(
                lambda step=step: scatter_copy(which, step).start()
            )

    def gather(which):
        parts, landing, sums, send, recv = shared[5 * which : 5 * which + 5]

        @pl.when(owner)
        def _():
            total = parts[rank].astype(F32)
            for step in range(1, ALL):
                scatter_copy(which, step).wait_recv()
            for step in range(1, ALL):
                total = total + landing[step].astype(F32)
            sums[rank] = total.astype(BF16)
            for step in range(1, ALL):
                gather_copy(which, step).start()

    def finish(which, out):
        sums = shared[5 * which + 2]
        for step in range(1, ALL):
            pl.when((rank - step + ALL) % ALL < PIECES)(
                lambda step=step: gather_copy(which, step).wait_recv()
            )
        out[...] = sums[0:PIECES].astype(F32)

    def settle(which):
        for step in range(1, ALL):
            pl.when((rank + step) % ALL < PIECES)(
                lambda step=step: scatter_copy(which, step).wait_send()
            )
            pl.when(owner)(lambda step=step: gather_copy(which, step).wait_send())

    lane = lax.broadcasted_iota(jnp.int32, (1, 128), 1)
    low = lane < 64
    even = lane % 2 == 0

    def grouped(total):
        total = total + pltpu.roll(total, 64, 1)
        return total + jnp.where(even, pltpu.roll(total, 127, 1), pltpu.roll(total, 1, 1))

    def frame_sums(first, second):
        rows = [jnp.sum(v.reshape(4, 4 * PAIRS, 128), axis=1) for v in (first, second)]
        pad = jnp.zeros((4, 128), F32)
        return jnp.concatenate([rows[0], pad]), jnp.concatenate([rows[1], pad])

    def put_stats(turn, first, second):
        a, b = frame_sums(first, second)
        stats[turn, OWN, 0:8] = a
        stats[turn, OWN, 8:16] = b

    for buf in (lat, cot, hid, err):
        buf[...] = jnp.zeros_like(buf)
    stats[...] = jnp.zeros_like(stats)
    lat[2:6, 1:5] = lat_ref[...]
    cot[2:6, 1:5] = cot_ref[...]
    mine = lat_ref[...].astype(F32)
    put_stats(0, mine, mine * mine)
    stats[0, OWN, 16:24] = ids_ref[...]

    barrier = pltpu.get_barrier_semaphore()

    def greet(target):
        pl.semaphore_signal(barrier, inc=1, device_id=target, device_id_type=MESH)

    if direct:
        for step in range(1, ALL):
            greet(around(step))
        pl.semaphore_wait(barrier, ALL - 1)
    else:
        for d, o in peers:
            guarded(within(d), lambda d=d, o=o: greet(device(d, o)))
        reached = jnp.minimum(me, REACH) + jnp.minimum(n_tm - 1 - me, REACH)
        pl.semaphore_wait(barrier, 2 * reached + 1)

    send_stats(0)
    send_halo("cot")
    send_halo("lat")

    g_one, b_one, g_two, b_two = (vec_ref[i : i + 1] for i in range(4))

    pair = lax.broadcasted_iota(jnp.int32, (6, PAIRS, 128), 1)
    image_row = lax.broadcasted_iota(jnp.int32, (6, PAIRS, 128), 0) + 4 * core
    inside = ((pair < n_cols // 2) & (image_row >= 1) & (image_row <= 8)).reshape(
        1, 6, PAIRS, 128
    )
    in_pair = lax.broadcasted_iota(jnp.int32, (1, 1, PAIRS, 128), 2) < n_cols // 2

    def windows(win, field):
        rows = 36 * PAIRS
        cur = field.reshape(rows, 128)
        side = jnp.where(low, pltpu.roll(cur, rows - 1, 0), pltpu.roll(cur, 1, 0))
        win[:, :, :, 0:128] = cur.reshape(6, 6, PAIRS, 128).astype(BF16)
        win[:, :, :, 128:256] = side.reshape(6, 6, PAIRS, 128).astype(BF16)

    def conv(win, weight, first, masks):
        total = None
        for lag in range(3):
            frame = 2 - lag if first else lag
            part = None
            for tap in range(3):
                patch = win[frame : frame + 4, tap : tap + 4].reshape(cells, 256)
                term = jnp.dot(
                    patch, weight[3 * lag + tap], preferred_element_type=F32
                )
                part = term if part is None else part + term
            part = part.reshape(4, 4, PAIRS, 128)
            if lag > 0:
                part = jnp.where(masks[lag], part, 0.0)
            total = part if total is None else total + part
        return jnp.where(in_pair, total, 0.0)

    def kernel_grad(win, grad, masks, out):
        for lag in range(3):
            kept = grad if lag == 0 else jnp.where(masks[lag], grad, 0.0)
            turned = kept.reshape(cells, 128).T.astype(BF16)
            for tap in range(3):
                patch = win[2 - lag : 6 - lag, tap : tap + 4].reshape(cells, 256)
                prod = jnp.dot(turned, patch, preferred_element_type=F32)
                a_lo, a_hi = prod[0:64, 0:128], prod[0:64, 128:256]
                b_lo, b_hi = prod[64:128, 0:128], prod[64:128, 128:256]
                later = a_lo + pltpu.roll(jnp.where(low, b_hi, b_lo), 64, 1)
                early = a_hi + pltpu.roll(b_lo, 64, 1)
                packed = jnp.where(low, pltpu.roll(early[0:32], 64, 1), early[32:64])
                index = 3 * (3 * lag + tap)
                out[index] = later[0:32].astype(out.dtype)
                out[index + 1] = later[32:64].astype(out.dtype)
                out[index + 2] = packed.astype(out.dtype)

    recv_stats(0)
    all_ids = stats[0, :, 16:24].reshape(SLOTS * 8, 128)
    before, own_ids, after = (
        stats[0, OWN - 2, 16:24], stats[0, OWN, 16:24], stats[0, OWN + 2, 16:24]
    )
    ids = [before[2:3], before[3:4]] + [own_ids[f : f + 1] for f in range(4)]
    ids = ids + [after[0:1], after[1:2]]
    match = [(all_ids == i).astype(F32) for i in ids]
    per_slot = float(4 * n_cols * 2)
    count = jnp.concatenate([jnp.sum(m, axis=0, keepdims=True) for m in match])
    count = jnp.maximum(count, 1.0) * per_slot

    def totals(turn):
        both = []
        for part in range(2):
            table = stats[turn, :, 8 * part : 8 * part + 8].reshape(SLOTS * 8, 128)
            rows = [jnp.sum(m * table, axis=0, keepdims=True) for m in match]
            both.append(grouped(jnp.concatenate(rows)) / count)
        return both

    def per_frame(rows, lo, hi):
        return rows[lo:hi].reshape(hi - lo, 1, 1, 128)

    def same(lag, direction):
        rows = [
            jnp.broadcast_to(
                (ids[2 + f] == ids[2 + f + direction * lag]).astype(F32).reshape(1, 1, 1, 128),
                (1, 1, 1, 128),
            )
            for f in range(4)
        ]
        return jnp.concatenate(rows, axis=0) > 0.5

    lags = [None, same(1, -1), same(2, -1)]
    leads = [None, same(1, 1), same(2, 1)]

    recv_halo("cot")
    windows(win_cot, cot[2:8].astype(F32))
    back_two = conv(win_cot, w2t_ref, False, leads)
    err[2:6, 1:5] = back_two
    send_halo("err")

    def moments(turn):
        mean, square = totals(turn)
        return mean, lax.rsqrt(jnp.maximum(square - mean * mean, 0.0) + EPSILON)

    mean_one, rstd_one = moments(0)
    recv_halo("lat")
    normed = (lat[0:6].astype(F32) - per_frame(mean_one, 0, 6)) * per_frame(rstd_one, 0, 6)
    z_value = normed * g_one + b_one
    windows(win_one, jnp.where(inside, z_value * jax.nn.sigmoid(z_value), 0.0))
    hidden = conv(win_one, w1_ref, True, lags).astype(BF16)
    hid[2:6, 1:5] = hidden
    wide = hidden.astype(F32)
    put_stats(1, wide, wide * wide)
    send_stats(1)
    send_halo("hid")

    recv_stats(1)
    mean_two, rstd_two = moments(1)
    recv_halo("hid")
    recv_halo("err")
    normed = (hid[2:8].astype(F32) - per_frame(mean_two, 2, 8)) * per_frame(rstd_two, 2, 8)
    z_value = normed * g_two + b_two
    sig = jax.nn.sigmoid(z_value)
    slope = err[2:8] * sig * (1.0 + z_value * (1.0 - sig)) * g_two
    core_slope = jnp.where(in_pair, slope[0:4, 1:5], 0.0)
    put_stats(2, core_slope, core_slope * normed[0:4, 1:5])
    send_stats(2)

    past = (hid[0:2].astype(F32) - per_frame(mean_two, 0, 2)) * per_frame(rstd_two, 0, 2)
    past_z = past * g_two + b_two
    act = jnp.concatenate([past_z * jax.nn.sigmoid(past_z), z_value[0:4] * sig[0:4]], axis=0)
    windows(win_two, jnp.where(inside, act, 0.0))
    out_ref[...] = (conv(win_two, w2_ref, True, lags) + lat_ref[...].astype(F32)).astype(BF16)
    kernel_grad(win_two, cot_ref[...].astype(F32), lags, shared[0] if direct else g2_ref)
    if direct:
        scatter(0)

    recv_stats(2)
    p_two, q_two = totals(2)
    grad_hidden = per_frame(rstd_two, 2, 8) * (
        slope - per_frame(p_two, 2, 8) - normed * per_frame(q_two, 2, 8)
    )
    grad_hidden = jnp.where(inside, grad_hidden, 0.0).astype(BF16).astype(F32)
    kernel_grad(win_one, grad_hidden[0:4, 1:5], lags, shared[5] if direct else g1_ref)
    if direct:
        scatter(1)
    windows(win_back, grad_hidden)
    back_one = conv(win_back, w1t_ref, False, leads)

    normed = (lat_ref[...].astype(F32) - per_frame(mean_one, 2, 6)) * per_frame(rstd_one, 2, 6)
    z_value = normed * g_one + b_one
    sig = jax.nn.sigmoid(z_value)
    slope = back_one * sig * (1.0 + z_value * (1.0 - sig)) * g_one
    put_stats(3, slope, slope * normed)
    send_stats(3)
    if direct:
        gather(0)
        gather(1)
    recv_stats(3)
    p_one, q_one = totals(3)
    branch = per_frame(rstd_one, 2, 6) * (
        slope - per_frame(p_one, 2, 6) - normed * per_frame(q_one, 2, 6)
    )
    gl_ref[...] = (cot_ref[...].astype(F32) + branch).astype(BF16)

    if direct:
        finish(0, g2_ref)
        finish(1, g1_ref)
        settle(0)
        settle(1)
    for turn in range(4):
        for d, o in peers:
            guarded(within(d), lambda d=d, o=o: stat_copy(turn, d, o).wait_send())
    for name in halos:
        for item in halos[name]:
            guarded(within(spans[item[2]][0]), lambda item=item: halo_copy(*item).wait_send())


def banded(kernel, flip):
    if flip:
        kernel = jnp.swapaxes(kernel[:, ::-1, ::-1], 3, 4)
    taps = kernel.reshape(9, 3, kernel.shape[3], kernel.shape[4])
    none = jnp.zeros_like(taps[:, :1])
    left = jnp.concatenate([taps[:, 1:], none, taps[:, :1]], axis=1)
    right = jnp.concatenate([taps, none], axis=1)
    return jnp.concatenate([left, right], axis=3).reshape(9, 256, 128)


def unpacked(packed):
    packed = packed.reshape(9, 96, 128)
    later = packed[:, 0:64].reshape(9, 64, 2, 64).transpose(0, 2, 3, 1)
    early = packed[:, 64:96].reshape(9, 32, 2, 64).transpose(0, 3, 2, 1).reshape(9, 1, 64, 64)
    return jnp.concatenate([early, later], axis=1).reshape(3, 3, 3, 64, 64)


def per_device(
    n_tm, latents, cotangent, kernel_one, kernel_two, gain_one, offset_one, gain_two, offset_two,
    clip_id,
):
    n_frames, n_rows, flat = latents.shape
    channels = gain_one.shape[0]
    n_cols = flat // channels

    def shaped(field):
        field = field.reshape(n_frames, n_rows, n_cols // 2, 128)
        return jnp.pad(field, ((0, 0), (0, 0), (0, PAIRS - n_cols // 2), (0, 0)))

    ids = jnp.broadcast_to(jnp.pad((clip_id + 1).astype(F32), (0, 4))[:, None], (8, 128))
    vec = jnp.stack([gain_one, offset_one, gain_two, offset_two])
    vec = jnp.pad(jnp.concatenate([vec, vec], axis=1), ((0, 4), (0, 0)))
    block = jax.ShapeDtypeStruct((4, 4, PAIRS, 128), BF16)
    grads = jax.ShapeDtypeStruct((PIECES, 32, 128), F32)
    direct = 2 * n_tm == ALL
    sharing = [
        pltpu.VMEM((ALL, 32, 128), BF16),
        pltpu.VMEM((ALL, 32, 128), BF16),
        pltpu.VMEM((ALL, 32, 128), BF16),
        pltpu.SemaphoreType.DMA((2, ALL)),
        pltpu.SemaphoreType.DMA((2, ALL)),
    ]
    out, grad_latent, grad_one, grad_two = pl.pallas_call(
        functools.partial(kernel, n_tm, n_cols),
        out_shape=(block, block, grads, grads),
        in_specs=[pl.BlockSpec(memory_space=pltpu.VMEM)] * 8,
        out_specs=[pl.BlockSpec(memory_space=pltpu.VMEM)] * 4,
        scratch_shapes=[
            pltpu.VMEM((8, 6, PAIRS, 128), BF16),
            pltpu.VMEM((8, 6, PAIRS, 128), BF16),
            pltpu.VMEM((8, 6, PAIRS, 128), BF16),
            pltpu.VMEM((8, 6, PAIRS, 128), F32),
            pltpu.VMEM((4, SLOTS, 24, 128), F32),
            pltpu.VMEM((6, 6, PAIRS, 256), BF16),
            pltpu.VMEM((6, 6, PAIRS, 256), BF16),
            pltpu.VMEM((6, 6, PAIRS, 256), BF16),
            pltpu.VMEM((6, 6, PAIRS, 256), BF16),
            pltpu.SemaphoreType.DMA((4, SLOTS)),
            pltpu.SemaphoreType.DMA((4, SLOTS)),
            pltpu.SemaphoreType.DMA((14,)),
            pltpu.SemaphoreType.DMA((14,)),
        ]
        + (2 * sharing if direct else []),
        compiler_params=pltpu.CompilerParams(
            collective_id=0, has_side_effects=True, vmem_limit_bytes=48 * 1024 * 1024
        ),
    )(
        shaped(latents), shaped(cotangent), ids,
        banded(kernel_one, False), banded(kernel_one, True),
        banded(kernel_two, False), banded(kernel_two, True), vec,
    )
    if not direct:
        grad_one, grad_two = lax.psum((grad_one, grad_two), ("tm", "rows"))

    def plain(field):
        return field[:, :, : n_cols // 2].reshape(n_frames, n_rows, flat)

    return (plain(out), plain(grad_latent), unpacked(grad_one), unpacked(grad_two))


def solution(mesh):
    return jax.shard_map(
        functools.partial(per_device, mesh.shape["tm"]),
        mesh=mesh,
        in_specs=(
            P("tm", "rows", None), P("tm", "rows", None), P(), P(), P(), P(), P(), P(), P("tm"),
        ),
        out_specs=(P("tm", "rows", None), P("tm", "rows", None), P(), P()),
        check_vma=False,
    )
```

time: 739 us -> 74.3 us (0.10); the launches traced: 728 us -> 73.8 us
  local copies, waits for them, and re-layouts: 314 us -> 9.66 us
  blocking collectives: 166 us -> 0 us
  waiting for transfers between devices: 134 us -> 0 us
  Pallas kernels: 0 us -> 60.5 us
  matrix products: 38 us -> 0 us
  starting transfers between devices: 35.2 us -> 0 us
  other arithmetic: 24.3 us -> 2.72 us
  between operations: 15.6 us -> 0.99 us
    psum x4 -> x0, blocking collectives: 166 us -> none  [clip_totals(): lax.psum((table_a, table_b, table_c), ('tm', 'rows'))]
    psum x1 -> x0, waiting for transfers between devices: 130 us -> none  [per_device(): grad_one, grad_two = lax.psum((grad_one, grad_two), ('tm', 'rows'))]
    mul x23 -> x0, local copies, waits for them, and re-layouts: 72.1 us -> none  [the longest x6 25.5 us: norm_forward(): normed = (grouped - mean_val[:, None, :, None]) * inv_std[:, None, :, None]]
    pallas_call x0 -> x1, Pallas kernels: none -> 60.5 us  [per_device(): pl.pallas_call(functools.partial(kernel, n_tm, n_cols), out_shape=(block,...]
    slice x23 -> x18, local copies, waits for them, and re-layouts: 57.3 us -> 0.41 us  [the longest x12 0.31 us: banded(): left = jnp.concatenate([taps[:, 1:], none, taps[:, :1]], axis=1)]
    concatenate x13 -> x3, local copies, waits for them, and re-layouts: 51.9 us -> 0.3 us  [the longest x2 0.29 us: unpacked(): return jnp.concatenate([early, later], axis=1).reshape(3, 3, 3, 64, 64)]
    sub x12 -> x0, local copies, waits for them, and re-layouts: 51.1 us -> none  [the longest x6 25.6 us: norm_backward(): grad_norm - p_term[:, None, :, None] - normed * q_term[:, None, :, None]]
    dot_general x36 -> x0, matrix products: 38 us -> none  [the longest x6 14.2 us: transposed_conv(): jnp.dot(patches, flipped, preferred_element_type=jnp.float32)]
  transfers between devices with their start and end apart: 15 -> 0, of which waited for: 2 -> 0; matrix products, arithmetic and copies ran while one was open for 28% -> 0% of each run, Pallas kernels for 0% -> 0%
where the time goes in v1:
time: 74.3 us; the launch traced here: 73.8 us
  Pallas kernels  60.5 us (81%)
  local copies, waits for them, and re-layouts  9.66 us (13%)
  other arithmetic  2.72 us (4%)
  between operations  0.99 us (1%)
    pallas_call x1, Pallas kernels, per_device(): pl.pallas_call(functools.partial(kernel, n_tm, n_cols), out_shape=(block,...  60.5 us
    unnamed x32, local copies, waits for them, and re-layouts  3.88 us

profile of v1, /device:TPU:0, one launch (start us, length us, event | category | flops | bytes accessed | tf_op | source)
XLA Modules:
  0.0 73.8 jit_solution(10596151995028629525)
XLA Ops:
  0.6 1.0 %rev.6 = bf16[3,3,3,64,64]{4,3,2,1,0:T(8,128)(2,1)S(1)} reverse(bf16[3,3,3,64,64]{4,3,2,1,0:T(8,128)(2,1)} %param.11), dimensions={1,2} | reverse | bytes 442368 | tf_op jit(solution)/shard_map/rev | solution.py:393
  1.7 0.2 copy.33
  2.0 0.7 %copy-done.4 = bf16[3,3,3,64,64]{4,3,2,1,0:T(8,128)(2,1)S(1)} copy-done((bf16[3,3,3,64,64]{4,3,2,1,0:T(8,128)(2,1)S(1)}, bf16[3,3,3,64,64]{4,3,2,1,0:T(8,128)(2,1)}, u32[]{:S(2)}) %copy-start.4) | copy-done | bytes 221208
  2.7 0.2 copy.36
  3.0 0.7 copy-done.5
  3.9 0.8 %copy-done.7 = bf16[9,3,64,64]{3,2,1,0:T(8,128)(2,1)S(1)} copy-done((bf16[9,3,64,64]{3,2,1,0:T(8,128)(2,1)S(1)}, bf16[9,3,64,64]{3,2,1,0:T(8,128)(2,1)}, u32[]{:S(2)}) %copy-start.7) | copy-done | bytes 221208
  4.8 0.1 slice-done
  4.9 0.2 copy-done.9
  5.0 0.1 slice-done.2
  5.2 1.3 %fusion.7 = (bf16[9,4,64,128]{3,2,1,0:T(8,128)(2,1)S(1)}, bf16[9,4,64,128]{3,2,1,0:T(8,128)(2,1)S(1)}, bf16[9,4,64,128]{3,2,1,0:T(8,128)(2,1)S(1)}, bf16[9,4,64,128]{3,2,1,0:T(8,128)(2,1)S(1)}) fusion(bf16[9,3,64,64]{3,2,1,0:T(8,128)(2,1)S(1)} %copy-done.9, bf16[9,1,64,64]{3,2,1,0:T(8,128)(2,1)S(1)} %slice-done.3, bf16[9,2,64,64]{3,2,1,0:T(8,128)(2,1)S(1)} %slice-done.2, ...), kind=kLoop, calls=%fused_computation.10 | loop fusion | flops 10027008 | bytes 4129792 | tf_op jit(solution)/shard_map/concatenate | solution.py:398
  6.6 1.0 %reshape.74 = bf16[4,4,40,128]{3,2,1,0:T(8,128)(2,1)S(1)} reshape(bf16[4,4,5120]{2,1,0:T(4,128)(2,1)} %param.10) | data formatting | bytes 327680 | tf_op jit(solution)/shard_map/reshape | solution.py:417
  7.8 0.1 fusion.8.vec_ref
  7.9 60.5 %shard_map.120 = (bf16[4,4,48,128]{3,2,1,0:T(8,128)(2,1)S(1)}, bf16[4,4,48,128]{3,2,1,0:T(8,128)(2,1)S(1)}, f32[27,32,128]{2,1,0:T(8,128)S(1)}, f32[27,32,128]{2,1,0:T(8,128)S(1)}) custom-call(bf16[4,4,48,128]{3,2,1,0:T(8,128)(2,1)S(1)} %pad.19.lat_ref, bf16[4,4,48,128]{3,2,1,0:T(8,128)(2,1)S(1)} %pad.20.cot_ref, f32[8,128]{1,0:T(8,128)S(1)} %broadcast_in_dim.2.ids_ref, ...), custom_call_target="tpu_custom_call" | custom-call | tf_op jit(solution)/shard_map/pallas_call | solution.py:433
  68.3 0.7 copy-done
  69.0 0.7 copy-done.2
  69.7 0.2 reshape.86
  69.9 0.1 copy.41
  70.1 0.2 reshape.89
  70.3 0.1 copy.44
  70.5 0.2 copy.45
  70.8 0.2 copy.46
  71.0 1.3 %pad_maximum_fusion = (f32[3,3,3,64,64]{4,3,2,1,0:T(8,128)}, f32[3,3,3,64,64]{4,3,2,1,0:T(8,128)}) fusion(f32[3,3,2,64,64]{4,3,2,1,0:T(8,128)S(1)} %bitcast.50, f32[3,3,1,64,64]{4,3,2,1,0:T(8,128)S(1)} %copy.41, f32[3,3,2,64,64]{4,3,2,1,0:T(8,128)S(1)} %bitcast.51, f32[3,3,1,64,64]{4,3,2,1,0:T(8,128)S(1)} %copy.44), kind=kLoop, calls=%fused_computation.5 | loop fusion | flops 221184 | bytes 1769472 | tf_op jit(solution)/shard_map/concatenate | solution.py:405
  72.4 0.7 reshape.83
  73.1 0.7 reshape.84
  (53 shorter events, 0.6 us)
Async XLA Ops:
  1.7 1.0 %copy-start.4 = (bf16[3,3,3,64,64]{4,3,2,1,0:T(8,128)(2,1)S(1)}, bf16[3,3,3,64,64]{4,3,2,1,0:T(8,128)(2,1)}, u32[]{:S(2)}) copy-start(bf16[3,3,3,64,64]{4,3,2,1,0:T(8,128)(2,1)} %param.12) | copy-start | bytes 663556
  1.9 1.1 %copy-start.6 = (bf16[9,3,64,64]{3,2,1,0:T(8,128)(2,1)}, bf16[9,3,64,64]{3,2,1,0:T(8,128)(2,1)S(1)}, u32[]{:S(2)}) copy-start(bf16[9,3,64,64]{3,2,1,0:T(8,128)(2,1)S(1)} %copy.33) | copy-start | bytes 663556
  2.7 1.0 %copy-start.5 = (bf16[3,3,3,64,64]{4,3,2,1,0:T(8,128)(2,1)S(1)}, bf16[3,3,3,64,64]{4,3,2,1,0:T(8,128)(2,1)}, u32[]{:S(2)}) copy-start(bf16[3,3,3,64,64]{4,3,2,1,0:T(8,128)(2,1)} %param.11) | copy-start | bytes 663556
  3.0 0.8 %copy-start.8 = (bf16[9,3,64,64]{3,2,1,0:T(8,128)(2,1)}, bf16[9,3,64,64]{3,2,1,0:T(8,128)(2,1)S(1)}, u32[]{:S(2)}) copy-start(bf16[9,3,64,64]{3,2,1,0:T(8,128)(2,1)S(1)} %copy.36) | copy-start | bytes 663556
  3.7 1.0 %copy-start.7 = (bf16[9,3,64,64]{3,2,1,0:T(8,128)(2,1)S(1)}, bf16[9,3,64,64]{3,2,1,0:T(8,128)(2,1)}, u32[]{:S(2)}) copy-start(bf16[9,3,64,64]{3,2,1,0:T(8,128)(2,1)} %copy-done.6) | copy-start | bytes 663556
  3.7 1.1 %slice-start = ((bf16[9,3,64,64]{3,2,1,0:T(8,128)(2,1)}), bf16[9,2,64,64]{3,2,1,0:T(8,128)(2,1)S(1)}, s32[]{:S(2)}) async-start(bf16[9,3,64,64]{3,2,1,0:T(8,128)(2,1)} %copy-done.6), calls=%async_computation | async-start | bytes 589824 | tf_op jit(solution)/shard_map/slice | solution.py:396
  3.7 1.1 %slice-start.1 = ((bf16[9,3,64,64]{3,2,1,0:T(8,128)(2,1)}), bf16[9,1,64,64]{3,2,1,0:T(8,128)(2,1)S(1)}, s32[]{:S(2)}) async-start(bf16[9,3,64,64]{3,2,1,0:T(8,128)(2,1)} %copy-done.6), calls=%async_computation.1 | async-start | bytes 294912 | tf_op jit(solution)/shard_map/slice | solution.py:396
  3.8 1.2 %copy-start.9 = (bf16[9,3,64,64]{3,2,1,0:T(8,128)(2,1)S(1)}, bf16[9,3,64,64]{3,2,1,0:T(8,128)(2,1)}, u32[]{:S(2)}) copy-start(bf16[9,3,64,64]{3,2,1,0:T(8,128)(2,1)} %copy-done.8) | copy-start | bytes 663556
  3.8 1.3 %slice-start.2 = ((bf16[9,3,64,64]{3,2,1,0:T(8,128)(2,1)}), bf16[9,2,64,64]{3,2,1,0:T(8,128)(2,1)S(1)}, s32[]{:S(2)}) async-start(bf16[9,3,64,64]{3,2,1,0:T(8,128)(2,1)} %copy-done.8), calls=%async_computation.2 | async-start | bytes 589824 | tf_op jit(solution)/shard_map/slice | solution.py:396
  3.8 1.3 %slice-start.3 = ((bf16[9,3,64,64]{3,2,1,0:T(8,128)(2,1)}), bf16[9,1,64,64]{3,2,1,0:T(8,128)(2,1)S(1)}, s32[]{:S(2)}) async-start(bf16[9,3,64,64]{3,2,1,0:T(8,128)(2,1)} %copy-done.8), calls=%async_computation.3 | async-start | bytes 294912 | tf_op jit(solution)/shard_map/slice | solution.py:396
  5.2 1.4 %copy-start.10 = (bf16[4,4,5120]{2,1,0:T(4,128)(2,1)S(1)}, bf16[4,4,5120]{2,1,0:T(4,128)(2,1)}, u32[]{:S(2)}) copy-start(bf16[4,4,5120]{2,1,0:T(4,128)(2,1)} %param.9) | copy-start | bytes 491524
  6.5 1.2 %copy-start.15 = (s32[4]{0:T(128)S(1)}, s32[4]{0:T(128)}, u32[]{:S(2)}) copy-start(s32[4]{0:T(128)} %param.17) | copy-start | bytes 52
  6.5 1.3 %copy-start.11 = (f32[64]{0:T(128)S(1)}, f32[64]{0:T(128)}, u32[]{:S(2)}) copy-start(f32[64]{0:T(128)} %param.16) | copy-start | bytes 772
  6.5 1.3 %copy-start.12 = (f32[64]{0:T(128)S(1)}, f32[64]{0:T(128)}, u32[]{:S(2)}) copy-start(f32[64]{0:T(128)} %param.15) | copy-start | bytes 772
  6.5 1.3 %copy-start.13 = (f32[64]{0:T(128)S(1)}, f32[64]{0:T(128)}, u32[]{:S(2)}) copy-start(f32[64]{0:T(128)} %param.14) | copy-start | bytes 772
  6.5 1.2 %copy-start.14 = (f32[64]{0:T(128)S(1)}, f32[64]{0:T(128)}, u32[]{:S(2)}) copy-start(f32[64]{0:T(128)} %param.13) | copy-start | bytes 772
  68.3 0.7 copy-start
  69.0 0.7 copy-start.2
  71.0 1.4 %copy-start.3 = (bf16[4,4,48,128]{3,2,1,0:T(8,128)(2,1)S(1)}, bf16[4,4,48,128]{3,2,1,0:T(8,128)(2,1)}, u32[]{:S(2)}) copy-start(bf16[4,4,48,128]{3,2,1,0:T(8,128)(2,1)} %copy-done.2) | copy-start | bytes 589828
  71.0 2.1 %copy-start.1 = (bf16[4,4,48,128]{3,2,1,0:T(8,128)(2,1)S(1)}, bf16[4,4,48,128]{3,2,1,0:T(8,128)(2,1)}, u32[]{:S(2)}) copy-start(bf16[4,4,48,128]{3,2,1,0:T(8,128)(2,1)} %copy-done) | copy-start | bytes 589828

commit v2 on v1

--- a/solution.py
+++ b/solution.py
@@ -19,12 +19,12 @@
 
 
 def kernel(
-    n_tm, n_cols, lat_ref, cot_ref, ids_ref, w1_ref, w1t_ref, w2_ref, w2t_ref, vec_ref,
+    n_tm, n_cols, lat_ref, cot_ref, ids_ref, k1_ref, k2_ref, vec_ref,
     out_ref, gl_ref, g1_ref, g2_ref,
-    lat, cot, hid, err, stats, win_one, win_two, win_cot, win_back,
+    w1_ref, w1t_ref, w2_ref, w2t_ref, lat, cot, hid, err, stats, win_one, win_two, win_cot, win_back,
     stat_send, stat_recv, halo_send, halo_recv, *shared,
 ):
-    direct = len(shared) > 0
+    direct = 2 * n_tm == ALL
     me = lax.axis_index("tm")
     core = lax.axis_index("rows")
     cells = 16 * PAIRS
@@ -157,13 +157,43 @@
             for step in range(1, ALL):
                 gather_copy(which, step).start()
 
+    def unpack(pieces, out):
+        for index in range(9):
+            rows = [pieces[3 * index + i].astype(F32) for i in range(3)]
+            turned = jnp.concatenate(rows + [jnp.zeros((32, 128), F32)]).T
+            early = turned[:, 64:96]
+            out[3 * index] = jnp.concatenate([early[0:64], early[64:128]], axis=1)
+            out[3 * index + 1] = turned[0:64, 0:64]
+            out[3 * index + 2] = turned[64:128, 0:64]
+
+    def band(source, ahead, back):
+        none = jnp.zeros((64, 64), F32)
+        for lag in range(3):
+            for tap in range(3):
+                first, second, third = (
+                    source[9 * lag + 3 * tap + j].astype(F32) for j in range(3)
+                )
+                blocks = [
+                    jnp.concatenate(two, axis=1).astype(BF16)
+                    for two in (
+                        (second, first), (third, second), (none, third), (first, none)
+                    )
+                ]
+                index, mirror = 3 * lag + tap, 3 * lag + 2 - tap
+                for i in range(4):
+                    ahead[index, 64 * i : 64 * i + 64] = blocks[i]
+                back[mirror, 0:64, 0:128] = blocks[0]
+                back[mirror, 0:64, 128:256] = blocks[2]
+                back[mirror, 64:128, 0:128] = blocks[1]
+                back[mirror, 64:128, 128:256] = blocks[3]
+
     def finish(which, out):
         sums = shared[5 * which + 2]
         for step in range(1, ALL):
             pl.when((rank - step + ALL) % ALL < PIECES)(
                 lambda step=step: gather_copy(which, step).wait_recv()
             )
-        out[...] = sums[0:PIECES].astype(F32)
+        unpack(sums, out)
 
     def settle(which):
         for step in range(1, ALL):
@@ -207,16 +237,19 @@
     if direct:
         for step in range(1, ALL):
             greet(around(step))
+        band(k1_ref, w1_ref, w1t_ref)
         pl.semaphore_wait(barrier, ALL - 1)
     else:
         for d, o in peers:
             guarded(within(d), lambda d=d, o=o: greet(device(d, o)))
+        band(k1_ref, w1_ref, w1t_ref)
         reached = jnp.minimum(me, REACH) + jnp.minimum(n_tm - 1 - me, REACH)
         pl.semaphore_wait(barrier, 2 * reached + 1)
 
     send_stats(0)
+    send_halo("lat")
     send_halo("cot")
-    send_halo("lat")
+    band(k2_ref, w2_ref, w2t_ref)
 
     g_one, b_one, g_two, b_two = (vec_ref[i : i + 1] for i in range(4))
 
@@ -241,8 +274,11 @@
             part = None
             for tap in range(3):
                 patch = win[frame : frame + 4, tap : tap + 4].reshape(cells, 256)
-                term = jnp.dot(
-                    patch, weight[3 * lag + tap], preferred_element_type=F32
+                term = lax.dot_general(
+                    patch,
+                    weight[3 * lag + tap],
+                    (((1,), (0 if first else 1,)), ((), ())),
+                    preferred_element_type=F32,
                 )
                 part = term if part is None else part + term
             part = part.reshape(4, 4, PAIRS, 128)
@@ -304,12 +340,6 @@
     lags = [None, same(1, -1), same(2, -1)]
     leads = [None, same(1, 1), same(2, 1)]
 
-    recv_halo("cot")
-    windows(win_cot, cot[2:8].astype(F32))
-    back_two = conv(win_cot, w2t_ref, False, leads)
-    err[2:6, 1:5] = back_two
-    send_halo("err")
-
     def moments(turn):
         mean, square = totals(turn)
         return mean, lax.rsqrt(jnp.maximum(square - mean * mean, 0.0) + EPSILON)
@@ -326,24 +356,27 @@
     send_stats(1)
     send_halo("hid")
 
+    recv_halo("cot")
+    windows(win_cot, cot[2:8].astype(F32))
+    back_two = conv(win_cot, w2t_ref, False, leads)
+    err[2:6, 1:5] = back_two
+    send_halo("err")
+
     recv_stats(1)
     mean_two, rstd_two = moments(1)
     recv_halo("hid")
-    recv_halo("err")
-    normed = (hid[2:8].astype(F32) - per_frame(mean_two, 2, 8)) * per_frame(rstd_two, 2, 8)
+    normed = (hid[...].astype(F32) - per_frame(mean_two, 0, 8)) * per_frame(rstd_two, 0, 8)
     z_value = normed * g_two + b_two
     sig = jax.nn.sigmoid(z_value)
+    windows(win_two, jnp.where(inside, z_value[0:6] * sig[0:6], 0.0))
+    out_ref[...] = (conv(win_two, w2_ref, True, lags) + lat_ref[...].astype(F32)).astype(BF16)
+    recv_halo("err")
+    normed, z_value, sig = normed[2:8], z_value[2:8], sig[2:8]
     slope = err[2:8] * sig * (1.0 + z_value * (1.0 - sig)) * g_two
     core_slope = jnp.where(in_pair, slope[0:4, 1:5], 0.0)
     put_stats(2, core_slope, core_slope * normed[0:4, 1:5])
     send_stats(2)
-
-    past = (hid[0:2].astype(F32) - per_frame(mean_two, 0, 2)) * per_frame(rstd_two, 0, 2)
-    past_z = past * g_two + b_two
-    act = jnp.concatenate([past_z * jax.nn.sigmoid(past_z), z_value[0:4] * sig[0:4]], axis=0)
-    windows(win_two, jnp.where(inside, act, 0.0))
-    out_ref[...] = (conv(win_two, w2_ref, True, lags) + lat_ref[...].astype(F32)).astype(BF16)
-    kernel_grad(win_two, cot_ref[...].astype(F32), lags, shared[0] if direct else g2_ref)
+    kernel_grad(win_two, cot_ref[...].astype(F32), lags, shared[0])
     if direct:
         scatter(0)
 
@@ -353,9 +386,10 @@
         slope - per_frame(p_two, 2, 8) - normed * per_frame(q_two, 2, 8)
     )
     grad_hidden = jnp.where(inside, grad_hidden, 0.0).astype(BF16).astype(F32)
-    kernel_grad(win_one, grad_hidden[0:4, 1:5], lags, shared[5] if direct else g1_ref)
+    kernel_grad(win_one, grad_hidden[0:4, 1:5], lags, shared[5 if direct else 1])
     if direct:
         scatter(1)
+        gather(0)
     windows(win_back, grad_hidden)
     back_one = conv(win_back, w1t_ref, False, leads)
 
@@ -366,8 +400,8 @@
     put_stats(3, slope, slope * normed)
     send_stats(3)
     if direct:
-        gather(0)
         gather(1)
+        finish(0, g2_ref)
     recv_stats(3)
     p_one, q_one = totals(3)
     branch = per_frame(rstd_one, 2, 6) * (
@@ -376,33 +410,18 @@
     gl_ref[...] = (cot_ref[...].astype(F32) + branch).astype(BF16)
 
     if direct:
-        finish(0, g2_ref)
         finish(1, g1_ref)
         settle(0)
         settle(1)
+    else:
+        unpack(shared[0], g2_ref)
+        unpack(shared[1], g1_ref)
     for turn in range(4):
         for d, o in peers:
             guarded(within(d), lambda d=d, o=o: stat_copy(turn, d, o).wait_send())
     for name in halos:
         for item in halos[name]:
             guarded(within(spans[item[2]][0]), lambda item=item: halo_copy(*item).wait_send())
-
-
-def banded(kernel, flip):
-    if flip:
-        kernel = jnp.swapaxes(kernel[:, ::-1, ::-1], 3, 4)
-    taps = kernel.reshape(9, 3, kernel.shape[3], kernel.shape[4])
-    none = jnp.zeros_like(taps[:, :1])
-    left = jnp.concatenate([taps[:, 1:], none, taps[:, :1]], axis=1)
-    right = jnp.concatenate([taps, none], axis=1)
-    return jnp.concatenate([left, right], axis=3).reshape(9, 256, 128)
-
-
-def unpacked(packed):
-    packed = packed.reshape(9, 96, 128)
-    later = packed[:, 0:64].reshape(9, 64, 2, 64).transpose(0, 2, 3, 1)
-    early = packed[:, 64:96].reshape(9, 32, 2, 64).transpose(0, 3, 2, 1).reshape(9, 1, 64, 64)
-    return jnp.concatenate([early, later], axis=1).reshape(3, 3, 3, 64, 64)
 
 
 def per_device(
@@ -421,7 +440,7 @@
     vec = jnp.stack([gain_one, offset_one, gain_two, offset_two])
     vec = jnp.pad(jnp.concatenate([vec, vec], axis=1), ((0, 4), (0, 0)))
     block = jax.ShapeDtypeStruct((4, 4, PAIRS, 128), BF16)
-    grads = jax.ShapeDtypeStruct((PIECES, 32, 128), F32)
+    grads = jax.ShapeDtypeStruct((27, 64, 64), F32)
     direct = 2 * n_tm == ALL
     sharing = [
         pltpu.VMEM((ALL, 32, 128), BF16),
@@ -433,9 +452,13 @@
     out, grad_latent, grad_one, grad_two = pl.pallas_call(
         functools.partial(kernel, n_tm, n_cols),
         out_shape=(block, block, grads, grads),
-        in_specs=[pl.BlockSpec(memory_space=pltpu.VMEM)] * 8,
+        in_specs=[pl.BlockSpec(memory_space=pltpu.VMEM)] * 6,
         out_specs=[pl.BlockSpec(memory_space=pltpu.VMEM)] * 4,
         scratch_shapes=[
+            pltpu.VMEM((9, 256, 128), BF16),
+            pltpu.VMEM((9, 128, 256), BF16),
+            pltpu.VMEM((9, 256, 128), BF16),
+            pltpu.VMEM((9, 128, 256), BF16),
             pltpu.VMEM((8, 6, PAIRS, 128), BF16),
             pltpu.VMEM((8, 6, PAIRS, 128), BF16),
             pltpu.VMEM((8, 6, PAIRS, 128), BF16),
@@ -450,14 +473,13 @@
             pltpu.SemaphoreType.DMA((14,)),
             pltpu.SemaphoreType.DMA((14,)),
         ]
-        + (2 * sharing if direct else []),
+        + (2 * sharing if direct else [pltpu.VMEM((PIECES, 32, 128), F32)] * 2),
         compiler_params=pltpu.CompilerParams(
             collective_id=0, has_side_effects=True, vmem_limit_bytes=48 * 1024 * 1024
         ),
     )(
         shaped(latents), shaped(cotangent), ids,
-        banded(kernel_one, False), banded(kernel_one, True),
-        banded(kernel_two, False), banded(kernel_two, True), vec,
+        kernel_one.reshape(27, 64, 64), kernel_two.reshape(27, 64, 64), vec,
     )
     if not direct:
         grad_one, grad_two = lax.psum((grad_one, grad_two), ("tm", "rows"))
@@ -465,7 +487,8 @@
     def plain(field):
         return field[:, :, : n_cols // 2].reshape(n_frames, n_rows, flat)
 
-    return (plain(out), plain(grad_latent), unpacked(grad_one), unpacked(grad_two))
+    shape = kernel_one.shape
+    return (plain(out), plain(grad_latent), grad_one.reshape(shape), grad_two.reshape(shape))
 
 
 def solution(mesh):

time: 74.3 us -> 68.6 us (0.923)
  local copies, waits for them, and re-layouts: 9.66 us -> 6.72 us
  other arithmetic: 2.72 us -> 0.08 us
    concatenate x2 -> x0, other arithmetic: 2.64 us -> none  [the longest x1 1.33 us: unpacked(): return jnp.concatenate([early, later], axis=1).reshape(3, 3, 3, 64, 64)]
    reshape x6 -> x0, local copies, waits for them, and re-layouts: 1.37 us -> none  [the longest x2 0.49 us: banded(): taps = kernel.reshape(9, 3, kernel.shape[3], kernel.shape[4])]
    rev x2 -> x0, local copies, waits for them, and re-layouts: 1.07 us -> none  [banded(): kernel = jnp.swapaxes(kernel[:, ::-1, ::-1], 3, 4)]
    unnamed x32 -> x18, local copies, waits for them, and re-layouts: 3.88 us -> 4.08 us
where the time goes in v2:
time: 68.6 us; the launch traced here: 68.3 us
  Pallas kernels  60.7 us (88%)
  local copies, waits for them, and re-layouts  6.72 us (10%)
  between operations  0.74 us (1%)
    pallas_call x1, Pallas kernels, per_device(): pl.pallas_call(functools.partial(kernel, n_tm, n_cols), out_shape=(block,...  60.7 us
    unnamed x18, local copies, waits for them, and re-layouts  4.08 us
    reshape x2, local copies, waits for them, and re-layouts, plain(): return field[:, :, :n_cols // 2].reshape(n_frames, n_rows, flat)  1.41 us

profile of v2, /device:TPU:0, one launch (start us, length us, event | category | flops | bytes accessed | tf_op | source)
XLA Modules:
  0.0 68.3 jit_solution(4765312799368699533)
XLA Ops:
  0.6 0.0 copy-start.7
  0.6 0.6 copy-done.7
  1.3 0.0 copy-start.3
  1.3 0.0 copy-start.4
  1.3 0.0 copy-start.5
  1.3 0.0 copy-start.6
  1.3 0.1 broadcast_in_dim.2.ids_ref
  1.4 0.5 copy-done.3
  2.0 0.0 copy-done.4
  2.0 0.0 copy-done.5
  2.0 0.0 copy-done.6
  2.0 0.1 fusion.vec_ref
  2.1 1.0 %reshape.33 = bf16[4,4,40,128]{3,2,1,0:T(8,128)(2,1)S(1)} reshape(bf16[4,4,5120]{2,1,0:T(4,128)(2,1)} %param.9) | data formatting | bytes 327680 | tf_op jit(solution)/shard_map/reshape | solution.py:436
  3.1 0.0 copy-start
  3.1 0.0 copy-start.1
  3.2 0.0 copy-done.2
  3.2 0.1 reshape.34
  3.3 0.9 %copy-done = bf16[3,3,3,64,64]{4,3,2,1,0:T(8,128)(2,1)S(1)} copy-done((bf16[3,3,3,64,64]{4,3,2,1,0:T(8,128)(2,1)S(1)}, bf16[3,3,3,64,64]{4,3,2,1,0:T(8,128)(2,1)}, u32[]{:S(2)}) %copy-start) | copy-done | bytes 221208
  4.1 0.1 copy-done.1
  4.3 60.7 %shard_map.120 = (bf16[4,4,48,128]{3,2,1,0:T(8,128)(2,1)S(1)}, bf16[4,4,48,128]{3,2,1,0:T(8,128)(2,1)S(1)}, f32[27,64,64]{2,1,0:T(8,128)S(1)}, f32[27,64,64]{2,1,0:T(8,128)S(1)}) custom-call(bf16[4,4,48,128]{3,2,1,0:T(8,128)(2,1)S(1)} %pad.15.lat_ref, bf16[4,4,48,128]{3,2,1,0:T(8,128)(2,1)S(1)} %pad.16.cot_ref, f32[8,128]{1,0:T(8,128)S(1)} %broadcast_in_dim.2.ids_ref, ...), custom_call_target="tpu_custom_call" | custom-call | tf_op jit(solution)/shard_map/pallas_call | solution.py:452
  65.0 0.7 %reshape.37 = bf16[4,4,5120]{2,1,0:T(4,128)(2,1)} reshape(bf16[4,4,40,128]{3,2,1,0:T(8,128)(2,1)S(1)} %slice.6) | data formatting | bytes 327680 | tf_op jit(solution)/shard_map/reshape | solution.py:488
  65.7 0.7 %reshape.38 = bf16[4,4,5120]{2,1,0:T(4,128)(2,1)} reshape(bf16[4,4,40,128]{3,2,1,0:T(8,128)(2,1)S(1)} %slice.7) | data formatting | bytes 327680 | tf_op jit(solution)/shard_map/reshape | solution.py:488
  66.4 0.9 %copy.15 = f32[3,3,3,64,64]{4,3,2,1,0:T(8,128)} copy(f32[3,3,3,64,64]{4,3,2,1,0:T(8,128)S(1)} %bitcast.13) | data formatting | bytes 884736
  67.3 0.9 %copy.16 = f32[3,3,3,64,64]{4,3,2,1,0:T(8,128)} copy(f32[3,3,3,64,64]{4,3,2,1,0:T(8,128)S(1)} %bitcast.12) | data formatting | bytes 884736
  (7 shorter events, 0.1 us)
Async XLA Ops:
  0.6 0.7 copy-start.7
  1.3 0.7 copy-start.3
  1.3 0.7 copy-start.4
  1.3 0.7 copy-start.5
  1.3 0.7 copy-start.6
  2.1 1.1 %copy-start.2 = (bf16[4,4,5120]{2,1,0:T(4,128)(2,1)S(1)}, bf16[4,4,5120]{2,1,0:T(4,128)(2,1)}, u32[]{:S(2)}) copy-start(bf16[4,4,5120]{2,1,0:T(4,128)(2,1)} %param.10) | copy-start | bytes 491524
  3.1 1.0 %copy-start = (bf16[3,3,3,64,64]{4,3,2,1,0:T(8,128)(2,1)S(1)}, bf16[3,3,3,64,64]{4,3,2,1,0:T(8,128)(2,1)}, u32[]{:S(2)}) copy-start(bf16[3,3,3,64,64]{4,3,2,1,0:T(8,128)(2,1)} %param.11) | copy-start | bytes 663556
  3.1 1.1 %copy-start.1 = (bf16[3,3,3,64,64]{4,3,2,1,0:T(8,128)(2,1)S(1)}, bf16[3,3,3,64,64]{4,3,2,1,0:T(8,128)(2,1)}, u32[]{:S(2)}) copy-start(bf16[3,3,3,64,64]{4,3,2,1,0:T(8,128)(2,1)} %param.12) | copy-start | bytes 663556

commit v3 on v2

--- a/solution.py
+++ b/solution.py
@@ -290,7 +290,7 @@
     def kernel_grad(win, grad, masks, out):
         for lag in range(3):
             kept = grad if lag == 0 else jnp.where(masks[lag], grad, 0.0)
-            turned = kept.reshape(cells, 128).T.astype(BF16)
+            turned = kept.reshape(cells, 128).astype(BF16).T
             for tap in range(3):
                 patch = win[2 - lag : 6 - lag, tap : tap + 4].reshape(cells, 256)
                 prod = jnp.dot(turned, patch, preferred_element_type=F32)
@@ -410,9 +410,7 @@
     gl_ref[...] = (cot_ref[...].astype(F32) + branch).astype(BF16)
 
     if direct:
-        finish(1, g1_ref)
         settle(0)
-        settle(1)
     else:
         unpack(shared[0], g2_ref)
         unpack(shared[1], g1_ref)
@@ -422,6 +420,9 @@
     for name in halos:
         for item in halos[name]:
             guarded(within(spans[item[2]][0]), lambda item=item: halo_copy(*item).wait_send())
+    if direct:
+        finish(1, g1_ref)
+        settle(1)
 
 
 def per_device(

time: 68.6 us -> 68.4 us (level)
  no operation moved by 1% of the time
where the time goes in v3:
time: 68.4 us; the launch traced here: 68.1 us
  Pallas kernels  60.5 us (88%)
  local copies, waits for them, and re-layouts  6.72 us (10%)
  between operations  0.74 us (1%)
    pallas_call x1, Pallas kernels, per_device(): pl.pallas_call(functools.partial(kernel, n_tm, n_cols), out_shape=(block,...  60.5 us
    unnamed x18, local copies, waits for them, and re-layouts  4.08 us
    reshape x2, local copies, waits for them, and re-layouts, plain(): return field[:, :, :n_cols // 2].reshape(n_frames, n_rows, flat)  1.41 us

profile of v3, /device:TPU:0, one launch (start us, length us, event | category | flops | bytes accessed | tf_op | source)
XLA Modules:
  0.0 68.1 jit_solution(2328333752137067718)
XLA Ops:
  0.6 0.0 copy-start.7
  0.6 0.6 copy-done.7
  1.3 0.0 copy-start.3
  1.3 0.0 copy-start.4
  1.3 0.0 copy-start.5
  1.3 0.0 copy-start.6
  1.3 0.1 broadcast_in_dim.2.ids_ref
  1.4 0.5 copy-done.3
  2.0 0.0 copy-done.4
  2.0 0.0 copy-done.5
  2.0 0.0 copy-done.6
  2.0 0.1 fusion.vec_ref
  2.1 1.0 %reshape.33 = bf16[4,4,40,128]{3,2,1,0:T(8,128)(2,1)S(1)} reshape(bf16[4,4,5120]{2,1,0:T(4,128)(2,1)} %param.9) | data formatting | bytes 327680 | tf_op jit(solution)/shard_map/reshape | solution.py:437
  3.1 0.0 copy-start
  3.1 0.0 copy-start.1
  3.2 0.0 copy-done.2
  3.2 0.1 reshape.34
  3.3 0.9 %copy-done = bf16[3,3,3,64,64]{4,3,2,1,0:T(8,128)(2,1)S(1)} copy-done((bf16[3,3,3,64,64]{4,3,2,1,0:T(8,128)(2,1)S(1)}, bf16[3,3,3,64,64]{4,3,2,1,0:T(8,128)(2,1)}, u32[]{:S(2)}) %copy-start) | copy-done | bytes 221208
  4.1 0.1 copy-done.1
  4.3 60.5 %shard_map.120 = (bf16[4,4,48,128]{3,2,1,0:T(8,128)(2,1)S(1)}, bf16[4,4,48,128]{3,2,1,0:T(8,128)(2,1)S(1)}, f32[27,64,64]{2,1,0:T(8,128)S(1)}, f32[27,64,64]{2,1,0:T(8,128)S(1)}) custom-call(bf16[4,4,48,128]{3,2,1,0:T(8,128)(2,1)S(1)} %pad.15.lat_ref, bf16[4,4,48,128]{3,2,1,0:T(8,128)(2,1)S(1)} %pad.16.cot_ref, f32[8,128]{1,0:T(8,128)S(1)} %broadcast_in_dim.2.ids_ref, ...), custom_call_target="tpu_custom_call" | custom-call | tf_op jit(solution)/shard_map/pallas_call | solution.py:453
  64.8 0.7 %reshape.37 = bf16[4,4,5120]{2,1,0:T(4,128)(2,1)} reshape(bf16[4,4,40,128]{3,2,1,0:T(8,128)(2,1)S(1)} %slice.6) | data formatting | bytes 327680 | tf_op jit(solution)/shard_map/reshape | solution.py:489
  65.5 0.7 %reshape.38 = bf16[4,4,5120]{2,1,0:T(4,128)(2,1)} reshape(bf16[4,4,40,128]{3,2,1,0:T(8,128)(2,1)S(1)} %slice.7) | data formatting | bytes 327680 | tf_op jit(solution)/shard_map/reshape | solution.py:489
  66.2 0.9 %copy.15 = f32[3,3,3,64,64]{4,3,2,1,0:T(8,128)} copy(f32[3,3,3,64,64]{4,3,2,1,0:T(8,128)S(1)} %bitcast.13) | data formatting | bytes 884736
  67.2 0.9 %copy.16 = f32[3,3,3,64,64]{4,3,2,1,0:T(8,128)} copy(f32[3,3,3,64,64]{4,3,2,1,0:T(8,128)S(1)} %bitcast.12) | data formatting | bytes 884736
  (7 shorter events, 0.1 us)
Async XLA Ops:
  0.6 0.7 copy-start.7
  1.3 0.7 copy-start.3
  1.3 0.7 copy-start.4
  1.3 0.7 copy-start.5
  1.3 0.7 copy-start.6
  2.1 1.1 %copy-start.2 = (bf16[4,4,5120]{2,1,0:T(4,128)(2,1)S(1)}, bf16[4,4,5120]{2,1,0:T(4,128)(2,1)}, u32[]{:S(2)}) copy-start(bf16[4,4,5120]{2,1,0:T(4,128)(2,1)} %param.10) | copy-start | bytes 491524
  3.1 1.0 %copy-start = (bf16[3,3,3,64,64]{4,3,2,1,0:T(8,128)(2,1)S(1)}, bf16[3,3,3,64,64]{4,3,2,1,0:T(8,128)(2,1)}, u32[]{:S(2)}) copy-start(bf16[3,3,3,64,64]{4,3,2,1,0:T(8,128)(2,1)} %param.11) | copy-start | bytes 663556
  3.1 1.1 %copy-start.1 = (bf16[3,3,3,64,64]{4,3,2,1,0:T(8,128)(2,1)S(1)}, bf16[3,3,3,64,64]{4,3,2,1,0:T(8,128)(2,1)}, u32[]{:S(2)}) copy-start(bf16[3,3,3,64,64]{4,3,2,1,0:T(8,128)(2,1)} %param.12) | copy-start | bytes 663556
